TPU v7x, 128 devices: a whole 4x4x4 slice. The times are simulated.
128 devices in a mesh: req: 16 (over y_hi, x, core), head: 8 (over y_lo, z).
Axes of the slice: x: 4, y: 4 (y_hi: 2, y_lo: 2; y = y_hi * 2 + y_lo), z: 4, core: 2. Of those that a mesh axis runs over, the one named last changes fastest.
Arguments:
- hidden: bfloat16 [512, 16, 2048], P('req', None, 'head'), may hold values from -6 to 6
- w_zx: bfloat16 [2048, 2, 4096], P(None, None, 'head'), may hold values from -0.125 to 0.125
- w_bc: bfloat16 [2048, 256], replicated, may hold values from -0.125 to 0.125
- w_dt: bfloat16 [2048, 64], P(None, 'head'), may hold values from -0.125 to 0.125
- conv_x_w: float32 [5, 4096], P(None, 'head'), may hold values from -3 to 3
- conv_bc_w: float32 [5, 256], replicated, may hold values from -3 to 3
- dt_bias: float32 [64], P('head'), may hold values from -4 to 0.5
- a_log: float32 [64], P('head'), may hold values from 0 to 2.5
- d_skip: float32 [64], P('head'), may hold values from 0.5 to 1.5
- norm_gain: float32 [4096], P('head'), may hold values from 0.1 to 1.9
- w_out: bfloat16 [4096, 2048], P('head'), may hold values from -0.09375 to 0.09375
- ssm_state: float32 [512, 64, 64, 128], P('req', 'head'), may hold values from -3 to 3
- conv_x_state: float32 [512, 3, 4096], P('req', None, 'head'), may hold values from -6 to 6
- conv_bc_state: float32 [512, 3, 256], P('req'), may hold values from -6 to 6
- slot: int32 [512], replicated, may hold values from 0 to 511, as said below
- lengths: int32 [512], replicated, may hold values from 0 to 16
- accepted: int32 [512], replicated, may hold values from 0 to 16
Outputs:
- out: bfloat16 [512, 16, 2048], P('req', None, 'head')
- new_state: float32 [512, 64, 64, 128], P('req', 'head')
- new_conv_x: float32 [512, 3, 4096], P('req', None, 'head')
- new_conv_bc: float32 [512, 3, 256], P('req')
Inputs may be any that keep to these rules, and one draw needn't show every extreme that they name: slot is a permutation of the pool rows; the requests of each aligned block of 32 requests have exactly 2 pool rows in each aligned block of 32 pool rows.
All inputs are finite; a program needn't handle non-finite values.
Results may differ from a plain program's by a relative error of at most 0.0082.
Values may be sent and summed in bfloat16 or wider, within the bound.
No kernel may reach another device: no remote copies, remote signals or barrier semaphores. Data moves between devices by JAX's collectives and lax.ppermute only.
A program may use at most 128 MiB of HBM per device.

v0:
```python
import jax
import jax.numpy as jnp
from jax import lax
from jax.sharding import PartitionSpec as P

highest = lax.Precision.HIGHEST


def conv_step(previous, inputs, taps):
    window = jnp.concatenate([previous, inputs.astype(jnp.float32)], axis=1)
    tail = taps.shape[0] - 1
    steps = inputs.shape[1]
    total = taps[tail] + taps[0] * window[:, 0:steps]
    for tap in range(1, tail):
        total = total + taps[tap] * window[:, tap : tap + steps]
    return (jax.nn.silu(total).astype(jnp.bfloat16), window)


def keep_rows(window, counted, tail):
    picks = counted[:, None] + jnp.arange(tail, dtype=jnp.int32)[None, :]
    return jnp.take_along_axis(window, picks[:, :, None], axis=1)


def scan_block(x_conv, bc_conv, dt_in, states, counted, dt_bias, a_log, d_skip):
    heads = states.shape[1]
    nstate = states.shape[3]
    blocks, steps, chans = x_conv.shape
    headdim = chans // heads
    xh = x_conv.astype(jnp.float32).reshape(blocks, steps, heads, headdim)
    bmat = bc_conv[..., :nstate].astype(jnp.float32)
    cmat = bc_conv[..., nstate:].astype(jnp.float32)
    step_size = jax.nn.softplus(dt_in.astype(jnp.float32) + dt_bias)
    rate = step_size * -jnp.exp(a_log)
    cumul = jnp.cumsum(rate, axis=1)
    carried = jnp.exp(cumul)[..., None] * jnp.einsum(
        "bhpn,btn->bthp", states, cmat, precision=highest
    )
    inner = jnp.einsum("btn,bsn->bts", cmat, bmat, precision=highest)
    places = jnp.arange(steps, dtype=jnp.int32)
    lower = (places[:, None] >= places[None, :])[None, :, :, None]
    spread = cumul[:, :, None, :] - cumul[:, None, :, :]
    factor = jnp.where(lower, jnp.exp(jnp.where(lower, spread, 0.0)), 0.0)
    factor = factor * inner[..., None] * step_size[:, None, :, :]
    within = jnp.einsum("btsh,bshp->bthp", factor, xh, precision=highest)
    mixed = (
        (carried + within + d_skip[:, None] * xh).reshape(blocks, steps, chans).astype(jnp.bfloat16)
    )
    live = (places[None, :] < counted[:, None])[..., None]
    total = jnp.sum(jnp.where(live, rate, 0.0), axis=1)
    remain = jnp.where(live, total[:, None, :] - cumul, 0.0)
    scaled = jnp.where(live, jnp.exp(remain) * step_size, 0.0)
    updated = jnp.exp(total)[:, :, None, None] * states
    updated = updated + jnp.einsum("bsh,bshp,bsn->bhpn", scaled, xh, bmat, precision=highest)
    return (mixed, updated)


def advance(
    x_pre,
    bc_pre,
    dt_pre,
    conv_x_prev,
    conv_bc_prev,
    states,
    counted,
    conv_x_w,
    conv_bc_w,
    dt_bias,
    a_log,
    d_skip,
):
    tail = conv_x_prev.shape[1]
    x_conv, x_window = conv_step(conv_x_prev, x_pre, conv_x_w)
    bc_conv, bc_window = conv_step(conv_bc_prev, bc_pre, conv_bc_w)
    mixed, updated = scan_block(x_conv, bc_conv, dt_pre, states, counted, dt_bias, a_log, d_skip)
    return (mixed, updated, keep_rows(x_window, counted, tail), keep_rows(bc_window, counted, tail))


def per_device(
    hidden,
    w_zx,
    w_bc,
    w_dt,
    conv_x_w,
    conv_bc_w,
    dt_bias,
    a_log,
    d_skip,
    norm_gain,
    w_out,
    ssm_state,
    conv_x_state,
    conv_bc_state,
    slot,
    lengths,
    accepted,
):
    local_requests, steps, width_part = hidden.shape
    width = w_zx.shape[0]
    local_inner = w_zx.shape[2]
    bc_cols = w_bc.shape[1]
    stacked = jnp.concatenate([w_zx.reshape(width, 2 * local_inner), w_bc, w_dt], axis=1)
    piece = lax.all_gather(hidden, "head", axis=2, tiled=True)
    projected = jnp.dot(
        piece.reshape(-1, piece.shape[2]), stacked, preferred_element_type=jnp.float32
    )
    projected = projected.astype(jnp.bfloat16).reshape(local_requests, steps, -1)
    gate_in = projected[..., :local_inner]
    x_in = projected[..., local_inner : 2 * local_inner]
    bc_in = projected[..., 2 * local_inner : 2 * local_inner + bc_cols]
    dt_in = projected[..., 2 * local_inner + bc_cols :]
    myself = lax.axis_index("req")
    peers = lax.axis_size("req")
    per_peer = local_requests // peers
    slot_blocks = slot.reshape(peers, local_requests)
    owner_blocks = slot_blocks // local_requests
    local_rows = slot_blocks % local_requests
    by_owner = jnp.argsort(owner_blocks, axis=1, stable=True)
    my_order = lax.dynamic_index_in_dim(by_owner, myself, 0, keepdims=False)
    undo_order = jnp.argsort(my_order)
    selected = lax.dynamic_slice_in_dim(by_owner, myself * per_peer, per_peer, 1)
    arrive_rows = jnp.take_along_axis(local_rows, selected, axis=1).reshape(local_requests)
    to_pool = jnp.argsort(arrive_rows)
    counted = jnp.minimum(accepted, lengths)
    counted_blocks = counted.reshape(peers, local_requests)
    my_lengths = lax.dynamic_index_in_dim(
        lengths.reshape(peers, local_requests), myself, 0, keepdims=False
    )
    outgoing = (
        jnp.take(ssm_state, arrive_rows, axis=0),
        jnp.take(conv_x_state, arrive_rows, axis=0),
        jnp.take(conv_bc_state, arrive_rows, axis=0),
    )
    states_in, conv_x_in, conv_bc_in = (
        lax.all_to_all(outgoing[0], "req", split_axis=0, concat_axis=0, tiled=True),
        lax.all_to_all(outgoing[1], "req", split_axis=0, concat_axis=0, tiled=True),
        lax.all_to_all(outgoing[2], "req", split_axis=0, concat_axis=0, tiled=True),
    )
    my_counted = jnp.take(
        lax.dynamic_index_in_dim(counted_blocks, myself, 0, keepdims=False), my_order, axis=0
    )
    mixed_sorted, states_out, conv_x_out, conv_bc_out = advance(
        jnp.take(x_in, my_order, axis=0),
        jnp.take(bc_in, my_order, axis=0),
        jnp.take(dt_in, my_order, axis=0),
        conv_x_in,
        conv_bc_in,
        states_in,
        my_counted,
        conv_x_w,
        conv_bc_w,
        dt_bias,
        a_log,
        d_skip,
    )
    mixed = jnp.take(mixed_sorted, undo_order, axis=0)
    back_states, back_conv_x, back_conv_bc = (
        lax.all_to_all(states_out, "req", split_axis=0, concat_axis=0, tiled=True),
        lax.all_to_all(conv_x_out, "req", split_axis=0, concat_axis=0, tiled=True),
        lax.all_to_all(conv_bc_out, "req", split_axis=0, concat_axis=0, tiled=True),
    )
    new_state = jnp.take(back_states, to_pool, axis=0)
    new_conv_x = jnp.take(back_conv_x, to_pool, axis=0)
    new_conv_bc = jnp.take(back_conv_bc, to_pool, axis=0)
    gated = mixed.astype(jnp.float32) * jax.nn.silu(gate_in.astype(jnp.float32))
    squares = lax.psum(jnp.sum(gated * gated, axis=-1), "head")
    meansq = squares / (local_inner * lax.axis_size("head"))
    normed = (gated * lax.rsqrt(meansq + 1e-05)[..., None] * norm_gain).astype(jnp.bfloat16)
    partial_out = jnp.dot(
        normed.reshape(-1, local_inner), w_out, preferred_element_type=jnp.float32
    ).reshape(local_requests, steps, width)
    summed = lax.psum_scatter(partial_out, "head", scatter_dimension=2, tiled=True)
    places = jnp.arange(steps, dtype=jnp.int32)
    valid = places[None, :] < my_lengths[:, None]
    out = jnp.where(valid[..., None], summed, 0.0).astype(jnp.bfloat16)
    return (out, new_state, new_conv_x, new_conv_bc)


def solution(mesh):
    in_specs = (
        P("req", None, "head"),
        P(None, None, "head"),
        P(),
        P(None, "head"),
        P(None, "head"),
        P(),
        P("head"),
        P("head"),
        P("head"),
        P("head"),
        P("head", None),
        P("req", "head", None, None),
        P("req", None, "head"),
        P("req", None, None),
        P(),
        P(),
        P(),
    )
    out_specs = (
        P("req", None, "head"),
        P("req", "head", None, None),
        P("req", None, "head"),
        P("req", None, None),
    )
    return jax.shard_map(
        per_device, mesh=mesh, in_specs=in_specs, out_specs=out_specs, check_vma=False
    )
```

profile of v0, /device:TPU:1, one launch (start us, length us, event | category | flops | bytes accessed | tf_op | source)
XLA Modules:
  0.0 478.6 jit_solution(8611803134680669130)
XLA Ops:
  7.2 0.8 min.3
  8.1 0.8 reshape.276
  9.0 0.8 sort.48
  10.0 1.6 sort.49
  14.9 0.8 copy_select_fusion
  15.7 8.4 %all-to-all-start = ((f32[32,3,256]{2,1,0:T(4,128)}), f32[32,3,256]{2,1,0:T(4,128)S(1)}, u32[]{:S(2)}, u32[]{:S(2)}) async-start(f32[32,3,256]{2,1,0:T(4,128)} %copy_select_fusion), calls=%async_computation | async-start | bytes 262144 | tf_op jit(solution)/shard_map/all_to_all | solution.py:136
  24.1 0.8 gather_fusion.8
  25.1 0.8 copy.86
  25.9 7.9 %gather_fusion.7 = f32[32,8,64,128]{3,2,1,0:T(8,128)} fusion(f32[32,8,64,128]{3,2,1,0:T(8,128)} %param.36, s32[1024]{0:T(1024)S(1)} %pad_clamp_fusion.3), kind=kCustom, calls=%fused_computation.1.clone | custom fusion | bytes 16777344 | tf_op jit(solution)/shard_map/jit(_take)/gather | solution.py:129
  34.4 7.2 %all-to-all-start.2 = ((f32[32,3,512]{2,1,0:T(4,128)}), f32[32,3,512]{2,1,0:T(4,128)S(1)}, u32[]{:S(2)}, u32[]{:S(2)}) async-start(f32[32,3,512]{2,1,0:T(4,128)} %copy.86), calls=%async_computation.2 | async-start | bytes 524288 | tf_op jit(solution)/shard_map/all_to_all | solution.py:135
  41.6 8.8 %broadcast_select_fusion.1 = f32[32,8,64,128]{3,2,1,0:T(8,128)} fusion(f32[32,8,64,128]{3,2,1,0:T(8,128)} %gather_fusion.7, pred[32]{0:T(512)(128)(4,1)S(1)} %get-tuple-element.47), kind=kLoop, calls=%fused_computation.22 | loop fusion | flops 2097152 | bytes 16777248 | tf_op jit(solution)/shard_map/jit(_take)/select_n | solution.py:129
  50.5 0.7 copy-done.5
  51.2 7.2 %all-to-all-start.1 = ((f32[32,8,64,128]{3,2,1,0:T(8,128)}), f32[32,8,64,128]{3,2,1,0:T(8,128)}, u32[]{:S(2)}, u32[]{:S(2)}) async-start(f32[32,8,64,128]{3,2,1,0:T(8,128)} %broadcast_select_fusion.1), calls=%async_computation.1 | async-start | bytes 16777216 | tf_op jit(solution)/shard_map/all_to_all | solution.py:134
  59.7 5.4 %copy.101 = bf16[256,8,2,512]{3,1,2,0:T(8,128)(2,1)} copy(bf16[256,8,2,512]{3,2,1,0:T(2,128)(2,1)} %bitcast.56) | data formatting | bytes 8388608
  68.7 104.9 %all-gather.2.cloned.1.call-done = bf16[32,16,2048]{2,1,0:T(8,128)(2,1)} async-done(((bf16[32,16,256]{2,1,0:T(8,128)(2,1)}), bf16[32,16,2048]{2,1,0:T(8,128)(2,1)}) %all-gather.2.cloned.1.call-update) | async-done | bytes 2097168 | tf_op jit(solution)/shard_map/all_gather | solution.py:102
  173.6 7.6 %fusion.9 = bf16[512,1288]{0,1:T(8,128)(2,1)} fusion(bf16[512,2048]{1,0:T(8,128)(2,1)} %bitcast.68, bf16[2048,8]{1,0:T(8,128)(2,1)S(1)} %copy.77, bf16[2048,256]{1,0:T(8,128)(2,1)} %param.27, bf16[2048,1024]{1,0:T(8,128)(2,1)} %bitcast.57), kind=kOutput, calls=%fused_computation.28 | convolution fusion | flops 2717618176 | bytes 8691712 | tf_op jit(solution)/shard_map/dot_general | solution.py:103
  181.2 2.3 copy.78
  183.5 0.8 slice.116
  184.9 0.9 slice.125
  185.8 1.6 copy.100
  187.4 2.2 gather_fusion
  189.6 1.7 copy.80
  191.4 1.2 select_reduce_fusion
  193.8 2.4 gather_fusion.1
  196.2 1.1 select_convert_fusion.2
  197.3 0.8 copy-done.4
  198.1 1.0 pad_maximum_fusion.1
  199.1 1.1 copy.95
  200.1 2.2 gather_fusion.5
  203.0 2.6 gather_fusion.9
  205.6 1.2 select_convert_fusion
  207.0 1.9 copy.94
  208.8 2.9 gather_fusion.4
  211.8 1.8 reshape.381
  213.5 2.4 multiply_convert_fusion.1
  215.9 1.6 reshape.281
  217.6 2.1 multiply_select_fusion
  219.7 1.1 copy.93
  220.8 1.8 copy.81
  222.6 1.8 copy.89
  224.4 0.8 copy.87
  225.2 1.7 broadcast_select_fusion.6
  226.9 2.4 multiply_convert_fusion.3
  229.5 1.8 broadcast_select_fusion.3
  231.3 2.9 fusion.16
  234.2 13.3 %all-to-all-start.5 = ((f32[32,3,256]{2,1,0:T(4,128)}), f32[32,3,256]{2,1,0:T(4,128)}, u32[]{:S(2)}, u32[]{:S(2)}) async-start(f32[32,3,256]{2,1,0:T(4,128)} %broadcast_select_fusion.6), calls=%async_computation.6 | async-start | bytes 262144 | tf_op jit(solution)/shard_map/all_to_all | solution.py:159
  247.6 13.9 %fusion.13 = bf16[32,16,8,64]{3,1,2,0:T(8,128)(2,1)S(1)} fusion(f32[32,8,64,16]{2,3,1,0:T(8,128)} %fusion.16, f32[32,8,64,128]{3,2,1,0:T(8,128)} %all-to-all-done.1, f32[8]{0:T(128)S(1)} %copy-done.25, f32[32,16,8]{1,2,0:T(8,128)} %copy.81, bf16[32,16,8,64]{3,2,1,0:T(8,128)(2,1)S(1)} %reshape.281, bf16[32,16,256]{2,1,0:T(8,128)(2,1)S(1)} %multiply_convert_fusion.3), kind=kOutput, calls=%fused_computation.32 | convolution fusion | flops 404226048 | bytes 11158016 | tf_op jit(solution)/shard_map/bhpn,btn->bthp/dot_general | solution.py:35
  261.5 1.2 copy.92
  262.7 2.6 convert_element_type.54
  265.3 2.6 gather_fusion.10
  267.8 13.1 %multiply_add_fusion = f32[32,8,64,128]{3,2,1,0:T(8,128)} fusion(f32[32,8,64,128]{3,2,1,0:T(8,128)} %all-to-all-done.1, f32[32,8]{1,0:T(8,128)S(1)} %copy-done.14, f32[32,16,8]{1,2,0:T(8,128)S(1)} %copy.93, bf16[32,16,8,64]{3,2,1,0:T(8,128)(2,1)S(1)} %reshape.281, bf16[32,16,256]{2,1,0:T(8,128)(2,1)S(1)} %multiply_convert_fusion.3), kind=kOutput, calls=%fused_computation.14 | convolution fusion | flops 407371776 | bytes 18104320 | tf_op jit(solution)/shard_map/bsh,bshp,bsn->bhpn/dot_general | solution.py:53
  280.9 1.5 multiply_reduce_fusion
  282.5 26.1 %psum.7 = f32[32,16]{1,0:T(8,128)S(1)} all-reduce(f32[32,16]{1,0:T(8,128)S(1)} %multiply_reduce_fusion), channel_id=1, replica_groups=mesh['req'=16,'head'=8] {'head'}, use_global_device_ids=true, to_apply=%region_4.9 | all-reduce | flops 512 | bytes 4096 | tf_op jit(solution)/shard_map/psum | solution.py:165
  308.6 15.1 %all-to-all-start.4 = ((f32[32,3,512]{2,1,0:T(4,128)}), f32[32,3,512]{2,1,0:T(4,128)S(1)}, u32[]{:S(2)}, u32[]{:S(2)}) async-start(f32[32,3,512]{2,1,0:T(4,128)} %broadcast_select_fusion.3), calls=%async_computation.5 | async-start | bytes 524288 | tf_op jit(solution)/shard_map/all_to_all | solution.py:158
  323.7 8.6 %all-to-all-done.4 = f32[32,3,512]{2,1,0:T(4,128)S(1)} async-done(((f32[32,3,512]{2,1,0:T(4,128)}), f32[32,3,512]{2,1,0:T(4,128)S(1)}, u32[]{:S(2)}, u32[]{:S(2)}) %all-to-all-start.4) | async-done | bytes 196640 | tf_op jit(solution)/shard_map/all_to_all | solution.py:158
  332.4 5.3 %all-to-all-start.3 = ((f32[32,8,64,128]{3,2,1,0:T(8,128)}), f32[32,8,64,128]{3,2,1,0:T(8,128)}, u32[]{:S(2)}, u32[]{:S(2)}) async-start(f32[32,8,64,128]{3,2,1,0:T(8,128)} %multiply_add_fusion), calls=%async_computation.4 | async-start | bytes 16777216 | tf_op jit(solution)/shard_map/all_to_all | solution.py:157
  337.7 4.6 fusion.14
  343.0 1.6 sort.50
  344.7 1.5 gather_fusion.13
  347.9 0.7 copy.96
  348.6 103.6 %all-to-all-done.3 = f32[32,8,64,128]{3,2,1,0:T(8,128)} async-done(((f32[32,8,64,128]{3,2,1,0:T(8,128)}), f32[32,8,64,128]{3,2,1,0:T(8,128)}, u32[]{:S(2)}, u32[]{:S(2)}) %all-to-all-start.3) | async-done | bytes 8388640 | tf_op jit(solution)/shard_map/all_to_all | solution.py:157
  452.3 8.0 %gather_fusion.11 = f32[32,8,64,128]{3,2,1,0:T(8,128)} fusion(f32[32,8,64,128]{3,2,1,0:T(8,128)} %all-to-all-done.3, s32[1024]{0:T(1024)S(1)} %pad_clamp_fusion), kind=kCustom, calls=%fused_computation.5.clone | custom fusion | bytes 16777344 | tf_op jit(solution)/shard_map/jit(_take)/gather | solution.py:161
  460.2 8.9 %broadcast_select_fusion = f32[32,8,64,128]{3,2,1,0:T(8,128)} fusion(f32[32,8,64,128]{3,2,1,0:T(8,128)} %gather_fusion.11, pred[32]{0:T(512)(128)(4,1)S(1)} %compare_and_fusion), kind=kLoop, calls=%fused_computation.21 | loop fusion | flops 2097152 | bytes 16777248 | tf_op jit(solution)/shard_map/jit(_take)/select_n | solution.py:161
  469.7 1.9 select_convert_fusion.1
  (116 shorter events, 15.3 us)
Async XLA Ops:
  7.2 330.5 %copy-start = (bf16[512,2048]{1,0:T(8,128)(2,1)S(1)}, bf16[512,2048]{1,0:T(8,128)(2,1)}, u32[]{:S(2)}) copy-start(bf16[512,2048]{1,0:T(8,128)(2,1)} %param.35) | copy-start | bytes 6291460
  11.6 1.3 copy-start.17
  11.8 2.4 copy-start.2
  12.5 11.6 %copy-start.1 = (f32[32,3,512]{2,0,1:T(8,128)S(1)}, f32[32,3,512]{2,0,1:T(8,128)}, u32[]{:S(2)}) copy-start(f32[32,3,512]{2,0,1:T(8,128)} %param.37) | copy-start | bytes 589828
  12.9 1.3 copy-start.19
  15.7 18.1 %all-to-all-start = ((f32[32,3,256]{2,1,0:T(4,128)}), f32[32,3,256]{2,1,0:T(4,128)S(1)}, u32[]{:S(2)}, u32[]{:S(2)}) async-start(f32[32,3,256]{2,1,0:T(4,128)} %copy_select_fusion), calls=%async_computation | async-start | bytes 262144 | tf_op jit(solution)/shard_map/all_to_all | solution.py:136
  33.8 0.6 copy-start.10
  34.4 16.1 %all-to-all-start.2 = ((f32[32,3,512]{2,1,0:T(4,128)}), f32[32,3,512]{2,1,0:T(4,128)S(1)}, u32[]{:S(2)}, u32[]{:S(2)}) async-start(f32[32,3,512]{2,1,0:T(4,128)} %copy.86), calls=%async_computation.2 | async-start | bytes 524288 | tf_op jit(solution)/shard_map/all_to_all | solution.py:135
  50.5 8.9 %copy-start.15 = (bf16[2048,8]{0,1:T(8,128)(2,1)S(1)}, bf16[2048,8]{0,1:T(8,128)(2,1)}, u32[]{:S(2)}) copy-start(bf16[2048,8]{0,1:T(8,128)(2,1)} %param.28) | copy-start | bytes 98308
  50.5 0.7 copy-start.5
  51.2 183.0 %all-to-all-start.1 = ((f32[32,8,64,128]{3,2,1,0:T(8,128)}), f32[32,8,64,128]{3,2,1,0:T(8,128)}, u32[]{:S(2)}, u32[]{:S(2)}) async-start(f32[32,8,64,128]{3,2,1,0:T(8,128)} %broadcast_select_fusion.1), calls=%async_computation.1 | async-start | bytes 16777216 | tf_op jit(solution)/shard_map/all_to_all | solution.py:134
  58.4 115.2 %all-gather.2.cloned.1.call-start = ((), (), s32[]{:S(2)}) async-start(), calls=%async_computation.7 | async-start | bytes 2359296 | tf_op jit(solution)/shard_map/all_gather | solution.py:102
  59.7 7.2 %copy-start.27 = (f32[8]{0:T(128)S(1)}, f32[8]{0:T(128)}, u32[]{:S(2)}) copy-start(f32[8]{0:T(128)} %param.32) | copy-start | bytes 100
  59.7 7.8 %copy-start.21 = (f32[5,256]{1,0:T(8,128)S(1)}, f32[5,256]{1,0:T(8,128)}, u32[]{:S(2)}) copy-start(f32[5,256]{1,0:T(8,128)} %param.30) | copy-start | bytes 15364
  59.7 8.4 %copy-start.18 = (f32[5,512]{1,0:T(8,128)S(1)}, f32[5,512]{1,0:T(8,128)}, u32[]{:S(2)}) copy-start(f32[5,512]{1,0:T(8,128)} %param.29) | copy-start | bytes 30724
  183.4 15.6 %copy-start.3 = (bf16[512,1288]{1,0:T(8,128)(2,1)}, bf16[512,1288]{1,0:T(8,128)(2,1)S(1)}, u32[]{:S(2)}) copy-start(bf16[512,1288]{1,0:T(8,128)(2,1)S(1)} %copy.78) | copy-start | bytes 3956740
  192.6 0.6 copy-start.11
  197.2 0.8 copy-start.4
  200.1 6.7 %copy-start.6 = (f32[32,3,512]{2,1,0:T(4,128)S(1)}, f32[32,3,512]{2,1,0:T(4,128)}, u32[]{:S(2)}) copy-start(f32[32,3,512]{2,1,0:T(4,128)} %copy-done.5) | copy-start | bytes 589828
  211.8 5.8 %copy-start.7 = (bf16[32,16,8]{2,0,1:T(8,128)(2,1)S(1)}, bf16[32,16,8]{2,0,1:T(8,128)(2,1)}, u32[]{:S(2)}) copy-start(bf16[32,16,8]{2,0,1:T(8,128)(2,1)} %copy.80) | copy-start | bytes 24580
  219.7 11.6 %copy-start.24 = (pred[16,16]{1,0:T(8,128)(4,1)S(1)}, pred[16,16]{1,0:T(8,128)(4,1)}, u32[]{:S(2)}) copy-start(pred[16,16]{1,0:T(8,128)(4,1)} %iota_compare_fusion.2) | copy-start | bytes 772
  225.2 6.1 %copy-start.12 = (f32[32,16,8]{1,2,0:T(8,128)S(1)}, f32[32,16,8]{1,2,0:T(8,128)}, u32[]{:S(2)}) copy-start(f32[32,16,8]{1,2,0:T(8,128)} %copy.89) | copy-start | bytes 49156
  225.2 6.1 %copy-start.13 = (f32[32,16,8]{1,2,0:T(8,128)S(1)}, f32[32,16,8]{1,2,0:T(8,128)}, u32[]{:S(2)}) copy-start(f32[32,16,8]{1,2,0:T(8,128)} %copy.87) | copy-start | bytes 49156
  231.3 16.3 %copy-start.25 = (f32[8]{0:T(128)S(1)}, f32[8]{0:T(128)}, u32[]{:S(2)}) copy-start(f32[8]{0:T(128)} %param.33) | copy-start | bytes 100
  234.2 74.4 %all-to-all-start.5 = ((f32[32,3,256]{2,1,0:T(4,128)}), f32[32,3,256]{2,1,0:T(4,128)}, u32[]{:S(2)}, u32[]{:S(2)}) async-start(f32[32,3,256]{2,1,0:T(4,128)} %broadcast_select_fusion.6), calls=%async_computation.6 | async-start | bytes 262144 | tf_op jit(solution)/shard_map/all_to_all | solution.py:159
  261.4 6.4 %copy-start.14 = (f32[32,8]{1,0:T(8,128)S(1)}, f32[32,8]{1,0:T(8,128)}, u32[]{:S(2)}) copy-start(f32[32,8]{1,0:T(8,128)} %exp.49) | copy-start | bytes 3076
  267.8 13.1 %copy-start.8 = (bf16[32,16,512]{2,1,0:T(8,128)(2,1)S(1)}, bf16[32,16,512]{2,1,0:T(8,128)(2,1)}, u32[]{:S(2)}) copy-start(bf16[32,16,512]{2,1,0:T(8,128)(2,1)} %gather_fusion.10) | copy-start | bytes 1572868
  267.8 13.1 %copy-start.22 = (pred[32]{0:T(512)(128)(4,1)S(1)}, pred[32]{0:T(512)(128)(4,1)}, u32[]{:S(2)}) copy-start(pred[32]{0:T(512)(128)(4,1)} %get-tuple-element.46) | copy-start | bytes 100
  308.6 23.7 %all-to-all-start.4 = ((f32[32,3,512]{2,1,0:T(4,128)}), f32[32,3,512]{2,1,0:T(4,128)S(1)}, u32[]{:S(2)}, u32[]{:S(2)}) async-start(f32[32,3,512]{2,1,0:T(4,128)} %broadcast_select_fusion.3), calls=%async_computation.5 | async-start | bytes 524288 | tf_op jit(solution)/shard_map/all_to_all | solution.py:158
  323.7 14.0 %copy-start.9 = (bf16[32,16,512]{2,1,0:T(8,128)(2,1)S(1)}, bf16[32,16,512]{2,1,0:T(8,128)(2,1)}, u32[]{:S(2)}) copy-start(bf16[32,16,512]{2,1,0:T(8,128)(2,1)} %gather_fusion.10) | copy-start | bytes 1572868
  323.7 14.0 %copy-start.23 = (pred[32]{0:T(512)(128)(4,1)S(1)}, pred[32]{0:T(512)(128)(4,1)}, u32[]{:S(2)}) copy-start(pred[32]{0:T(512)(128)(4,1)} %get-tuple-element.46) | copy-start | bytes 100
  323.7 14.0 %copy-start.26 = (f32[512]{0:T(512)S(1)}, f32[512]{0:T(512)}, u32[]{:S(2)}) copy-start(f32[512]{0:T(512)} %param.34) | copy-start | bytes 6148
  332.4 119.9 %all-to-all-start.3 = ((f32[32,8,64,128]{3,2,1,0:T(8,128)}), f32[32,8,64,128]{3,2,1,0:T(8,128)}, u32[]{:S(2)}, u32[]{:S(2)}) async-start(f32[32,8,64,128]{3,2,1,0:T(8,128)} %multiply_add_fusion), calls=%async_computation.4 | async-start | bytes 16777216 | tf_op jit(solution)/shard_map/all_to_all | solution.py:157
  337.6 132.1 %reduce-scatter.2.cloned.1.call-start = ((), (), s32[]{:S(2)}) async-start(), calls=%async_computation.8 | async-start | bytes 4718592 | tf_op jit(solution)/shard_map/reduce_scatter | solution.py:171
  342.3 0.7 copy-start.16
  342.3 0.8 copy-start.20
Sparse Core Ops, SparseCore 0:
  60.8 112.7 all-gather.1
  342.4 127.2 reduce-scatter.1
where the time goes:
time: 487 us; the launch traced here: 479 us
  waiting for transfers between devices  218 us (45%)
  local copies, waits for them, and re-layouts  75.2 us (15%)
  starting transfers between devices  56.6 us (12%)
  other arithmetic  45.3 us (9%)
  matrix products  42.2 us (9%)
  blocking collectives  26.1 us (5%)
  between operations  14.7 us (3%)
    all_gather x1, waiting for transfers between devices, per_device(): piece = lax.all_gather(hidden, 'head', axis=2, tiled=True)  105 us
    all_to_all x1, waiting for transfers between devices, per_device(): lax.all_to_all(states_out, 'req', split_axis=0, concat_axis=0, tiled=True)  104 us
    psum x1, blocking collectives, per_device(): squares = lax.psum(jnp.sum(gated * gated, axis=-1), 'head')  26.1 us
    all_to_all x1, starting transfers between devices, per_device(): lax.all_to_all(conv_x_out, 'req', split_axis=0, concat_axis=0, tiled=True)  15.1 us
    dot_general x1, matrix products, scan_block(): jnp.einsum('bhpn,btn->bthp', states, cmat, precision=highest)  13.9 us
    all_to_all x1, starting transfers between devices, per_device(): lax.all_to_all(conv_bc_out, 'req', split_axis=0, concat_axis=0, tiled=True)  13.3 us
    dot_general x1, matrix products, scan_block(): jnp.einsum('bsh,bshp,bsn->bhpn', scaled, xh, bmat, precision=highest)  13.1 us
    unnamed x61, local copies, waits for them, and re-layouts  12.2 us
  transfers between devices with their start and end apart: 8, of which 4 were waited for; matrix products, arithmetic and copies ran while one was open for 31% of the time, Pallas kernels for 0%

commit v1 on v0

--- a/solution.py
+++ b/solution.py
@@ -4,6 +4,11 @@
 from jax.sharding import PartitionSpec as P
 
 highest = lax.Precision.HIGHEST
+
+
+def all_by_exchange(block, axis, dim):
+    repeated = jnp.stack([block] * lax.axis_size(axis))
+    return jnp.concatenate(lax.all_to_all(repeated, axis, 0, 0), axis=dim)
 
 
 def conv_step(previous, inputs, taps):
@@ -99,7 +104,7 @@
     local_inner = w_zx.shape[2]
     bc_cols = w_bc.shape[1]
     stacked = jnp.concatenate([w_zx.reshape(width, 2 * local_inner), w_bc, w_dt], axis=1)
-    piece = lax.all_gather(hidden, "head", axis=2, tiled=True)
+    piece = all_by_exchange(hidden, "head", 2)
     projected = jnp.dot(
         piece.reshape(-1, piece.shape[2]), stacked, preferred_element_type=jnp.float32
     )

time: 487 us -> 438 us (0.90)
  waiting for transfers between devices: 218 us -> 172 us
  blocking collectives: 26.1 us -> 37.9 us
  starting transfers between devices: 56.6 us -> 46.4 us
    all_gather x1 -> x0, waiting for transfers between devices: 105 us -> none  [per_device(): piece = lax.all_gather(hidden, 'head', axis=2, tiled=True)]
    all_to_all x1, waiting for transfers between devices: 0.01 us -> 42.4 us  [per_device(): lax.all_to_all(outgoing[0], 'req', split_axis=0, concat_axis=0, tiled=True)]
    all_to_all x0 -> x1, blocking collectives: none -> 12.3 us  [per_device(): lax.all_to_all(outgoing[1], 'req', split_axis=0, concat_axis=0, tiled=True)]
    all_to_all x1, waiting for transfers between devices: 0.01 us -> 10 us  [all_by_exchange(): return jnp.concatenate(lax.all_to_all(repeated, axis, 0, 0), axis=dim)]
    all_to_all x1, waiting for transfers between devices: 0.01 us -> 6.5 us  [per_device(): lax.all_to_all(outgoing[2], 'req', split_axis=0, concat_axis=0, tiled=True)]
    all_to_all x1, starting transfers between devices: 13.3 us -> 7.05 us  [per_device(): lax.all_to_all(conv_bc_out, 'req', split_axis=0, concat_axis=0, tiled=True)]
    unnamed x61 -> x64, local copies, waits for them, and re-layouts: 12.2 us -> 10.1 us
  transfers between devices with their start and end apart: 8 -> 7, of which waited for: 4 -> 6; matrix products, arithmetic and copies ran while one was open for 31% -> 34% of each run, Pallas kernels for 0% -> 0%
where the time goes in v1:
time: 438 us; the launch traced here: 433 us
  waiting for transfers between devices  172 us (39%)
  local copies, waits for them, and re-layouts  77.3 us (18%)
  starting transfers between devices  46.4 us (11%)
  other arithmetic  45.4 us (10%)
  matrix products  39.1 us (9%)
  blocking collectives  37.9 us (9%)
  between operations  14.8 us (3%)
    all_to_all x1, waiting for transfers between devices, per_device(): lax.all_to_all(states_out, 'req', split_axis=0, concat_axis=0, tiled=True)  104 us
    all_to_all x1, waiting for transfers between devices, per_device(): lax.all_to_all(outgoing[0], 'req', split_axis=0, concat_axis=0, tiled=True)  42.4 us
    psum x1, blocking collectives, per_device(): squares = lax.psum(jnp.sum(gated * gated, axis=-1), 'head')  25.6 us
    all_to_all x1, starting transfers between devices, per_device(): lax.all_to_all(conv_x_out, 'req', split_axis=0, concat_axis=0, tiled=True)  14.9 us
    dot_general x1, matrix products, scan_block(): jnp.einsum('bhpn,btn->bthp', states, cmat, precision=highest)  13.9 us
    dot_general x1, matrix products, scan_block(): jnp.einsum('bsh,bshp,bsn->bhpn', scaled, xh, bmat, precision=highest)  13.1 us
    all_to_all x1, blocking collectives, per_device(): lax.all_to_all(outgoing[1], 'req', split_axis=0, concat_axis=0, tiled=True)  12.3 us
    unnamed x64, local copies, waits for them, and re-layouts  10.1 us
  transfers between devices with their start and end apart: 7, of which 6 were waited for; matrix products, arithmetic and copies ran while one was open for 34% of the time, Pallas kernels for 0%

profile of v1, /device:TPU:1, one launch (start us, length us, event | category | flops | bytes accessed | tf_op | source)
XLA Modules:
  0.0 432.6 jit_solution(7025657091842731608)
XLA Ops:
  7.2 0.8 min.3
  9.0 0.8 sort.48
  10.0 1.6 sort.49
  14.9 0.8 copy_select_fusion
  15.7 8.4 %all-to-all-start.1 = ((f32[32,3,256]{2,1,0:T(4,128)}), f32[32,3,256]{2,1,0:T(4,128)S(1)}, u32[]{:S(2)}, u32[]{:S(2)}) async-start(f32[32,3,256]{2,1,0:T(4,128)} %copy_select_fusion), calls=%async_computation.1 | async-start | bytes 262144 | tf_op jit(solution)/shard_map/all_to_all | solution.py:141
  24.2 0.8 gather_fusion.8
  25.3 6.5 %all-to-all-done.1 = f32[32,3,256]{2,1,0:T(4,128)S(1)} async-done(((f32[32,3,256]{2,1,0:T(4,128)}), f32[32,3,256]{2,1,0:T(4,128)S(1)}, u32[]{:S(2)}, u32[]{:S(2)}) %all-to-all-start.1) | async-done | bytes 98336 | tf_op jit(solution)/shard_map/all_to_all | solution.py:141
  31.8 12.3 %all_to_all.35 = f32[32,3,512]{2,1,0:T(4,128)} all-to-all(f32[32,3,512]{2,1,0:T(4,128)S(1)} %copy.87), channel_id=1, replica_groups=mesh['req'=16,'head'=8] {'req'}, dimensions={0} | all-to-all | bytes 393216 | tf_op jit(solution)/shard_map/all_to_all | solution.py:140
  44.1 1.5 stack.2
  45.6 5.1 %all-to-all-start = ((bf16[8,32,16,256]{3,2,1,0:T(8,128)(2,1)}), bf16[8,32,16,256]{3,2,1,0:T(8,128)(2,1)}, u32[]{:S(2)}, u32[]{:S(2)}) async-start(bf16[8,32,16,256]{3,2,1,0:T(8,128)(2,1)} %stack.2), calls=%async_computation | async-start | bytes 4194304 | tf_op jit(solution)/shard_map/all_to_all | solution.py:11
  50.7 7.9 %gather_fusion.7 = f32[32,8,64,128]{3,2,1,0:T(8,128)} fusion(f32[32,8,64,128]{3,2,1,0:T(8,128)} %param.36, s32[1024]{0:T(1024)S(1)} %pad_clamp_fusion.3), kind=kCustom, calls=%fused_computation.1.clone | custom fusion | bytes 16777344 | tf_op jit(solution)/shard_map/jit(_take)/gather | solution.py:134
  58.6 8.8 %broadcast_select_fusion.1 = f32[32,8,64,128]{3,2,1,0:T(8,128)} fusion(f32[32,8,64,128]{3,2,1,0:T(8,128)} %gather_fusion.7, pred[32]{0:T(512)(128)(4,1)S(1)} %get-tuple-element.47), kind=kLoop, calls=%fused_computation.22 | loop fusion | flops 2097152 | bytes 16777248 | tf_op jit(solution)/shard_map/jit(_take)/select_n | solution.py:134
  67.5 10.0 %all-to-all-done = bf16[8,32,16,256]{3,2,1,0:T(8,128)(2,1)} async-done(((bf16[8,32,16,256]{3,2,1,0:T(8,128)(2,1)}), bf16[8,32,16,256]{3,2,1,0:T(8,128)(2,1)}, u32[]{:S(2)}, u32[]{:S(2)}) %all-to-all-start) | async-done | bytes 2097184 | tf_op jit(solution)/shard_map/all_to_all | solution.py:11
  77.5 5.5 %all-to-all-start.2 = ((f32[32,8,64,128]{3,2,1,0:T(8,128)}), f32[32,8,64,128]{3,2,1,0:T(8,128)}, u32[]{:S(2)}, u32[]{:S(2)}) async-start(f32[32,8,64,128]{3,2,1,0:T(8,128)} %broadcast_select_fusion.1), calls=%async_computation.2 | async-start | bytes 16777216 | tf_op jit(solution)/shard_map/all_to_all | solution.py:139
  83.5 3.4 copy.102
  90.6 3.3 copy.78
  95.1 4.5 %fusion.9 = bf16[512,1288]{0,1:T(8,128)(2,1)} fusion(bf16[512,2048]{1,0:T(8,128)(2,1)S(1)} %bitcast.62, bf16[2048,8]{1,0:T(8,128)(2,1)S(1)} %copy.77, bf16[2048,256]{1,0:T(8,128)(2,1)S(1)} %copy-done.26, bf16[2048,1024]{1,0:T(8,128)(2,1)S(1)} %bitcast.61), kind=kOutput, calls=%fused_computation.28 | convolution fusion | flops 2717618176 | bytes 8691712 | tf_op jit(solution)/shard_map/dot_general | solution.py:108
  99.6 2.3 copy.79
  103.4 0.9 slice.125
  104.3 1.6 copy.101
  106.0 2.2 gather_fusion
  108.1 1.7 copy.81
  109.9 1.2 select_reduce_fusion
  112.3 2.4 gather_fusion.1
  114.7 1.1 select_convert_fusion.2
  115.7 0.8 copy-done.4
  116.5 1.0 pad_maximum_fusion.1
  117.5 1.0 copy.96
  118.6 2.2 gather_fusion.5
  121.4 2.6 gather_fusion.9
  124.0 1.2 select_convert_fusion
  125.4 1.9 copy.95
  127.3 3.0 gather_fusion.4
  130.3 1.8 reshape.383
  132.1 2.3 multiply_convert_fusion.1
  134.4 1.6 reshape.283
  136.1 2.1 multiply_select_fusion
  138.2 1.1 copy.94
  139.3 1.8 copy.82
  141.1 1.8 copy.90
  142.8 0.8 copy.88
  143.7 1.7 broadcast_select_fusion.6
  145.4 2.5 multiply_convert_fusion.3
  148.1 1.8 broadcast_select_fusion.3
  149.9 2.9 fusion.16
  152.8 42.4 %all-to-all-done.2 = f32[32,8,64,128]{3,2,1,0:T(8,128)} async-done(((f32[32,8,64,128]{3,2,1,0:T(8,128)}), f32[32,8,64,128]{3,2,1,0:T(8,128)}, u32[]{:S(2)}, u32[]{:S(2)}) %all-to-all-start.2) | async-done | bytes 8388640 | tf_op jit(solution)/shard_map/all_to_all | solution.py:139
  195.2 7.1 %all-to-all-start.6 = ((f32[32,3,256]{2,1,0:T(4,128)}), f32[32,3,256]{2,1,0:T(4,128)}, u32[]{:S(2)}, u32[]{:S(2)}) async-start(f32[32,3,256]{2,1,0:T(4,128)} %broadcast_select_fusion.6), calls=%async_computation.7 | async-start | bytes 262144 | tf_op jit(solution)/shard_map/all_to_all | solution.py:164
  202.3 13.9 %fusion.13 = bf16[32,16,8,64]{3,1,2,0:T(8,128)(2,1)S(1)} fusion(f32[32,8,64,16]{2,3,1,0:T(8,128)} %fusion.16, f32[32,8,64,128]{3,2,1,0:T(8,128)} %all-to-all-done.2, f32[8]{0:T(128)S(1)} %copy-done.25, f32[32,16,8]{1,2,0:T(8,128)} %copy.82, bf16[32,16,8,64]{3,2,1,0:T(8,128)(2,1)S(1)} %reshape.283, bf16[32,16,256]{2,1,0:T(8,128)(2,1)S(1)} %multiply_convert_fusion.3), kind=kOutput, calls=%fused_computation.32 | convolution fusion | flops 404226048 | bytes 11158016 | tf_op jit(solution)/shard_map/bhpn,btn->bthp/dot_general | solution.py:40
  216.2 1.2 copy.93
  217.4 2.6 convert_element_type.54
  220.0 2.6 gather_fusion.10
  222.5 13.1 %multiply_add_fusion = f32[32,8,64,128]{3,2,1,0:T(8,128)} fusion(f32[32,8,64,128]{3,2,1,0:T(8,128)} %all-to-all-done.2, f32[32,8]{1,0:T(8,128)S(1)} %copy-done.14, f32[32,16,8]{1,2,0:T(8,128)S(1)} %copy.94, bf16[32,16,8,64]{3,2,1,0:T(8,128)(2,1)S(1)} %reshape.283, bf16[32,16,256]{2,1,0:T(8,128)(2,1)S(1)} %multiply_convert_fusion.3), kind=kOutput, calls=%fused_computation.14 | convolution fusion | flops 407371776 | bytes 18104320 | tf_op jit(solution)/shard_map/bsh,bshp,bsn->bhpn/dot_general | solution.py:58
  235.6 1.5 multiply_reduce_fusion
  237.2 25.6 %psum.7 = f32[32,16]{1,0:T(8,128)S(1)} all-reduce(f32[32,16]{1,0:T(8,128)S(1)} %multiply_reduce_fusion), channel_id=1, replica_groups=mesh['req'=16,'head'=8] {'head'}, use_global_device_ids=true, to_apply=%region_4.9 | all-reduce | flops 512 | bytes 4096 | tf_op jit(solution)/shard_map/psum | solution.py:170
  262.7 14.9 %all-to-all-start.5 = ((f32[32,3,512]{2,1,0:T(4,128)}), f32[32,3,512]{2,1,0:T(4,128)S(1)}, u32[]{:S(2)}, u32[]{:S(2)}) async-start(f32[32,3,512]{2,1,0:T(4,128)} %broadcast_select_fusion.3), calls=%async_computation.6 | async-start | bytes 524288 | tf_op jit(solution)/shard_map/all_to_all | solution.py:163
  277.7 8.6 %all-to-all-done.5 = f32[32,3,512]{2,1,0:T(4,128)S(1)} async-done(((f32[32,3,512]{2,1,0:T(4,128)}), f32[32,3,512]{2,1,0:T(4,128)S(1)}, u32[]{:S(2)}, u32[]{:S(2)}) %all-to-all-start.5) | async-done | bytes 196640 | tf_op jit(solution)/shard_map/all_to_all | solution.py:163
  286.3 5.3 %all-to-all-start.4 = ((f32[32,8,64,128]{3,2,1,0:T(8,128)}), f32[32,8,64,128]{3,2,1,0:T(8,128)}, u32[]{:S(2)}, u32[]{:S(2)}) async-start(f32[32,8,64,128]{3,2,1,0:T(8,128)} %multiply_add_fusion), calls=%async_computation.5 | async-start | bytes 16777216 | tf_op jit(solution)/shard_map/all_to_all | solution.py:162
  291.7 4.5 %fusion.14 = f32[32,16,2048]{2,1,0:T(8,128)} fusion(bf16[512,2048]{1,0:T(8,128)(2,1)S(1)} %copy-done, f32[512]{0:T(512)S(1)} %copy-done.27, f32[32,16]{1,0:T(8,128)S(1)} %add_rsqrt_fusion, bf16[32,16,1288]{2,1,0:T(8,128)(2,1)} %bitcast.59, bf16[32,16,512]{2,1,0:T(8,128)(2,1)S(1)} %copy-done.8, pred[32]{0:T(512)(128)(4,1)S(1)} %copy-done.23), kind=kOutput, calls=%fused_computation.33 | convolution fusion | flops 1076625408 | bytes 7344160 | tf_op jit(solution)/shard_map/dot_general | solution.py:173
  297.0 1.6 sort.50
  298.7 1.5 gather_fusion.13
  302.6 103.6 %all-to-all-done.4 = f32[32,8,64,128]{3,2,1,0:T(8,128)} async-done(((f32[32,8,64,128]{3,2,1,0:T(8,128)}), f32[32,8,64,128]{3,2,1,0:T(8,128)}, u32[]{:S(2)}, u32[]{:S(2)}) %all-to-all-start.4) | async-done | bytes 8388640 | tf_op jit(solution)/shard_map/all_to_all | solution.py:162
  406.3 8.0 %gather_fusion.11 = f32[32,8,64,128]{3,2,1,0:T(8,128)} fusion(f32[32,8,64,128]{3,2,1,0:T(8,128)} %all-to-all-done.4, s32[1024]{0:T(1024)S(1)} %pad_clamp_fusion), kind=kCustom, calls=%fused_computation.5.clone | custom fusion | bytes 16777344 | tf_op jit(solution)/shard_map/jit(_take)/gather | solution.py:166
  414.2 8.9 %broadcast_select_fusion = f32[32,8,64,128]{3,2,1,0:T(8,128)} fusion(f32[32,8,64,128]{3,2,1,0:T(8,128)} %gather_fusion.11, pred[32]{0:T(512)(128)(4,1)S(1)} %compare_and_fusion), kind=kLoop, calls=%fused_computation.21 | loop fusion | flops 2097152 | bytes 16777248 | tf_op jit(solution)/shard_map/jit(_take)/select_n | solution.py:166
  423.7 1.9 select_convert_fusion.1
  (119 shorter events, 17.5 us)
Async XLA Ops:
  7.2 284.5 %copy-start = (bf16[512,2048]{1,0:T(8,128)(2,1)S(1)}, bf16[512,2048]{1,0:T(8,128)(2,1)}, u32[]{:S(2)}) copy-start(bf16[512,2048]{1,0:T(8,128)(2,1)} %param.35) | copy-start | bytes 6291460
  11.6 1.3 copy-start.17
  11.8 2.4 copy-start.2
  12.5 11.7 %copy-start.1 = (f32[32,3,512]{2,0,1:T(8,128)S(1)}, f32[32,3,512]{2,0,1:T(8,128)}, u32[]{:S(2)}) copy-start(f32[32,3,512]{2,0,1:T(8,128)} %param.37) | copy-start | bytes 589828
  12.9 1.3 copy-start.19
  14.9 29.1 %copy-start.10 = (bf16[32,16,256]{2,1,0:T(8,128)(2,1)S(1)}, bf16[32,16,256]{2,1,0:T(8,128)(2,1)}, u32[]{:S(2)}) copy-start(bf16[32,16,256]{2,1,0:T(8,128)(2,1)} %param.25) | copy-start | bytes 786436
  15.7 16.0 %all-to-all-start.1 = ((f32[32,3,256]{2,1,0:T(4,128)}), f32[32,3,256]{2,1,0:T(4,128)S(1)}, u32[]{:S(2)}, u32[]{:S(2)}) async-start(f32[32,3,256]{2,1,0:T(4,128)} %copy_select_fusion), calls=%async_computation.1 | async-start | bytes 262144 | tf_op jit(solution)/shard_map/all_to_all | solution.py:141
  31.8 13.8 %copy-start.9 = (f32[32,3,256]{2,1,0:T(4,128)}, f32[32,3,256]{2,1,0:T(4,128)S(1)}, u32[]{:S(2)}) copy-start(f32[32,3,256]{2,1,0:T(4,128)S(1)} %all-to-all-done.1) | copy-start | bytes 294916
  45.6 31.9 %all-to-all-start = ((bf16[8,32,16,256]{3,2,1,0:T(8,128)(2,1)}), bf16[8,32,16,256]{3,2,1,0:T(8,128)(2,1)}, u32[]{:S(2)}, u32[]{:S(2)}) async-start(bf16[8,32,16,256]{3,2,1,0:T(8,128)(2,1)} %stack.2), calls=%async_computation | async-start | bytes 4194304 | tf_op jit(solution)/shard_map/all_to_all | solution.py:11
  67.4 15.7 %copy-start.15 = (bf16[2048,8]{0,1:T(8,128)(2,1)S(1)}, bf16[2048,8]{0,1:T(8,128)(2,1)}, u32[]{:S(2)}) copy-start(bf16[2048,8]{0,1:T(8,128)(2,1)} %param.28) | copy-start | bytes 98308
  77.5 117.7 %all-to-all-start.2 = ((f32[32,8,64,128]{3,2,1,0:T(8,128)}), f32[32,8,64,128]{3,2,1,0:T(8,128)}, u32[]{:S(2)}, u32[]{:S(2)}) async-start(f32[32,8,64,128]{3,2,1,0:T(8,128)} %broadcast_select_fusion.1), calls=%async_computation.2 | async-start | bytes 16777216 | tf_op jit(solution)/shard_map/all_to_all | solution.py:139
  83.5 5.2 %copy-start.28 = (f32[8]{0:T(128)S(1)}, f32[8]{0:T(128)}, u32[]{:S(2)}) copy-start(f32[8]{0:T(128)} %param.32) | copy-start | bytes 100
  83.5 5.8 %copy-start.21 = (f32[5,256]{1,0:T(8,128)S(1)}, f32[5,256]{1,0:T(8,128)}, u32[]{:S(2)}) copy-start(f32[5,256]{1,0:T(8,128)} %param.30) | copy-start | bytes 15364
  83.5 6.4 %copy-start.18 = (f32[5,512]{1,0:T(8,128)S(1)}, f32[5,512]{1,0:T(8,128)}, u32[]{:S(2)}) copy-start(f32[5,512]{1,0:T(8,128)} %param.29) | copy-start | bytes 30724
  93.9 1.2 copy-start.26
  102.0 15.5 %copy-start.3 = (bf16[512,1288]{1,0:T(8,128)(2,1)}, bf16[512,1288]{1,0:T(8,128)(2,1)S(1)}, u32[]{:S(2)}) copy-start(bf16[512,1288]{1,0:T(8,128)(2,1)S(1)} %copy.79) | copy-start | bytes 3956740
  111.1 0.6 copy-start.11
  115.7 0.8 copy-start.4
  118.6 6.6 %copy-start.5 = (f32[32,3,512]{2,1,0:T(4,128)S(1)}, f32[32,3,512]{2,1,0:T(4,128)}, u32[]{:S(2)}) copy-start(f32[32,3,512]{2,1,0:T(4,128)} %all_to_all.35) | copy-start | bytes 589828
  130.3 5.8 %copy-start.6 = (bf16[32,16,8]{2,0,1:T(8,128)(2,1)S(1)}, bf16[32,16,8]{2,0,1:T(8,128)(2,1)}, u32[]{:S(2)}) copy-start(bf16[32,16,8]{2,0,1:T(8,128)(2,1)} %copy.81) | copy-start | bytes 24580
  138.2 11.7 %copy-start.24 = (pred[16,16]{1,0:T(8,128)(4,1)S(1)}, pred[16,16]{1,0:T(8,128)(4,1)}, u32[]{:S(2)}) copy-start(pred[16,16]{1,0:T(8,128)(4,1)} %iota_compare_fusion.2) | copy-start | bytes 772
  143.7 6.2 %copy-start.12 = (f32[32,16,8]{1,2,0:T(8,128)S(1)}, f32[32,16,8]{1,2,0:T(8,128)}, u32[]{:S(2)}) copy-start(f32[32,16,8]{1,2,0:T(8,128)} %copy.90) | copy-start | bytes 49156
  143.7 6.2 %copy-start.13 = (f32[32,16,8]{1,2,0:T(8,128)S(1)}, f32[32,16,8]{1,2,0:T(8,128)}, u32[]{:S(2)}) copy-start(f32[32,16,8]{1,2,0:T(8,128)} %copy.88) | copy-start | bytes 49156
  149.8 52.4 %copy-start.25 = (f32[8]{0:T(128)S(1)}, f32[8]{0:T(128)}, u32[]{:S(2)}) copy-start(f32[8]{0:T(128)} %param.33) | copy-start | bytes 100
  195.2 67.5 %all-to-all-start.6 = ((f32[32,3,256]{2,1,0:T(4,128)}), f32[32,3,256]{2,1,0:T(4,128)}, u32[]{:S(2)}, u32[]{:S(2)}) async-start(f32[32,3,256]{2,1,0:T(4,128)} %broadcast_select_fusion.6), calls=%async_computation.7 | async-start | bytes 262144 | tf_op jit(solution)/shard_map/all_to_all | solution.py:164
  216.1 6.4 %copy-start.14 = (f32[32,8]{1,0:T(8,128)S(1)}, f32[32,8]{1,0:T(8,128)}, u32[]{:S(2)}) copy-start(f32[32,8]{1,0:T(8,128)} %exp.49) | copy-start | bytes 3076
  222.5 13.1 %copy-start.7 = (bf16[32,16,512]{2,1,0:T(8,128)(2,1)S(1)}, bf16[32,16,512]{2,1,0:T(8,128)(2,1)}, u32[]{:S(2)}) copy-start(bf16[32,16,512]{2,1,0:T(8,128)(2,1)} %gather_fusion.10) | copy-start | bytes 1572868
  222.5 13.1 %copy-start.22 = (pred[32]{0:T(512)(128)(4,1)S(1)}, pred[32]{0:T(512)(128)(4,1)}, u32[]{:S(2)}) copy-start(pred[32]{0:T(512)(128)(4,1)} %get-tuple-element.46) | copy-start | bytes 100
  262.7 23.6 %all-to-all-start.5 = ((f32[32,3,512]{2,1,0:T(4,128)}), f32[32,3,512]{2,1,0:T(4,128)S(1)}, u32[]{:S(2)}, u32[]{:S(2)}) async-start(f32[32,3,512]{2,1,0:T(4,128)} %broadcast_select_fusion.3), calls=%async_computation.6 | async-start | bytes 524288 | tf_op jit(solution)/shard_map/all_to_all | solution.py:163
  277.7 14.0 %copy-start.8 = (bf16[32,16,512]{2,1,0:T(8,128)(2,1)S(1)}, bf16[32,16,512]{2,1,0:T(8,128)(2,1)}, u32[]{:S(2)}) copy-start(bf16[32,16,512]{2,1,0:T(8,128)(2,1)} %gather_fusion.10) | copy-start | bytes 1572868
  277.7 14.0 %copy-start.23 = (pred[32]{0:T(512)(128)(4,1)S(1)}, pred[32]{0:T(512)(128)(4,1)}, u32[]{:S(2)}) copy-start(pred[32]{0:T(512)(128)(4,1)} %get-tuple-element.46) | copy-start | bytes 100
  277.7 14.0 %copy-start.27 = (f32[512]{0:T(512)S(1)}, f32[512]{0:T(512)}, u32[]{:S(2)}) copy-start(f32[512]{0:T(512)} %param.34) | copy-start | bytes 6148
  286.3 119.9 %all-to-all-start.4 = ((f32[32,8,64,128]{3,2,1,0:T(8,128)}), f32[32,8,64,128]{3,2,1,0:T(8,128)}, u32[]{:S(2)}, u32[]{:S(2)}) async-start(f32[32,8,64,128]{3,2,1,0:T(8,128)} %multiply_add_fusion), calls=%async_computation.5 | async-start | bytes 16777216 | tf_op jit(solution)/shard_map/all_to_all | solution.py:162
  291.6 132.1 %reduce-scatter.2.cloned.1.call-start = ((), (), s32[]{:S(2)}) async-start(), calls=%async_computation.8 | async-start | bytes 4718592 | tf_op jit(solution)/shard_map/reduce_scatter | solution.py:176
  296.2 0.7 copy-start.16
  296.2 0.8 copy-start.20
Sparse Core Ops, SparseCore 0:
  296.4 127.2 reduce-scatter.1
